TPU v7x, 256 devices: a whole 4x4x8 slice. The times are simulated.
256 devices in a mesh: dp: 8 (over z), space: 32 (over x, y, core).
Axes of the slice: x: 4, y: 4, z: 8, core: 2. Of those that a mesh axis runs over, the one named last changes fastest.
Arguments:
- volume: bfloat16 [8, 32, 8, 16, 16, 256], P('dp', 'space'), may hold values from -6 to 6
- fine_filter: bfloat16 [3, 3, 3, 256, 256], P(None, None, None, 'dp'), may hold values from -0.078125 to 0.078125
- coarse_filter: bfloat16 [3, 3, 3, 256, 256], P(None, None, None, 'dp'), may hold values from -0.078125 to 0.078125
- fine_bias: float32 [256], replicated, may hold values from -3 to 3
- coarse_bias: float32 [256], replicated, may hold values from -3 to 3
Outputs:
- context: bfloat16 [8, 32, 8, 16, 16, 256], P('dp', 'space')
All inputs are finite; a program needn't handle non-finite values.
Results may differ from a plain program's by a relative error of at most 0.0047.
Values may be sent and summed in bfloat16 or wider, within the bound.
No kernel may reach another device: no remote copies, remote signals or barrier semaphores. Data moves between devices by JAX's collectives and lax.ppermute only.
A program may use at most 128 MiB of HBM per device.

v0:
```python
import jax
import jax.numpy as jnp
from jax import lax
from jax.sharding import PartitionSpec as P

X = 64
BX = 8


def filters(shard):
    return lax.all_gather(shard, "dp", axis=3, tiled=True)


def dense_taps(grid, weights, bias):
    items, length_x, length_y, length_z, channels = grid.shape
    padded = jnp.pad(grid, ((0, 0), (1, 1), (1, 1), (1, 1), (0, 0)))
    total = jnp.zeros(grid.shape, jnp.float32)
    for step_x in range(3):
        for step_y in range(3):
            window = padded[:, step_x : step_x + length_x, step_y : step_y + length_y]
            stacked = jnp.concatenate(
                [window[:, :, :, depth : depth + length_z] for depth in range(3)], axis=-1
            )
            total = total + jnp.dot(
                stacked,
                weights[step_x, step_y].reshape(3 * channels, channels),
                preferred_element_type=jnp.float32,
            )
    return (grid.astype(jnp.float32) + jax.nn.gelu(total + bias)).astype(jnp.bfloat16)


def fine_cosets(brick):
    size_x, size_y, size_z, channels = brick.shape
    split = brick.reshape(size_x // 4, 4, size_y // 4, 4, size_z // 4, 4, channels)
    return split.transpose(1, 3, 5, 0, 2, 4, 6).reshape(
        64, size_x // 4, size_y // 4, size_z // 4, channels
    )


def fine_bricks(cosets):
    count, along_u, along_v, along_w, channels = cosets.shape
    split = cosets.reshape(4, 4, 4, along_u, along_v, along_w, channels).transpose(
        3, 0, 4, 1, 5, 2, 6
    )
    return split.reshape(along_u * 4, along_v * 4, along_w * 4, channels)


def assemble(parts):
    items, devices, along_u, along_v, along_w, channels = parts.shape
    across_x = X // BX
    across_y = devices // across_x
    grid = parts.reshape(items, across_x, across_y, along_u, along_v, along_w, channels).transpose(
        0, 1, 3, 2, 4, 5, 6
    )
    return grid.reshape(items, across_x * along_u, across_y * along_v, along_w, channels)


def disassemble(grid, along_u, along_v):
    items, size_x, size_y, along_w, channels = grid.shape
    across_x = size_x // along_u
    across_y = size_y // along_v
    parts = grid.reshape(items, across_x, along_u, across_y, along_v, along_w, channels).transpose(
        0, 1, 3, 2, 4, 5, 6
    )
    return parts.reshape(1, items, across_x * across_y, along_u, along_v, along_w, channels)


def split_halves(grid):
    items, size_x, size_y, size_z, channels = grid.shape
    parts = grid.reshape(items, size_x // 2, 2, size_y // 2, 2, size_z // 2, 2, channels).transpose(
        0, 2, 4, 6, 1, 3, 5, 7
    )
    return parts.reshape(items * 8, size_x // 2, size_y // 2, size_z // 2, channels)


def join_halves(parts, items):
    count, half_x, half_y, half_z, channels = parts.shape
    grid = parts.reshape(items, 2, 2, 2, half_x, half_y, half_z, channels).transpose(
        0, 4, 1, 5, 2, 6, 3, 7
    )
    return grid.reshape(items, half_x * 2, half_y * 2, half_z * 2, channels)


def on_device(volume, fine_filter, coarse_filter, fine_bias, coarse_bias):
    brick = volume[0, 0]
    devices = lax.axis_size("space")
    fine_weights = filters(fine_filter)
    coarse_weights = filters(coarse_filter)
    cosets = fine_cosets(brick)
    outgoing = cosets.reshape((devices, 64 // devices, 1) + cosets.shape[1:])
    received = lax.all_to_all(outgoing, "space", split_axis=0, concat_axis=2, tiled=True)
    items = received.shape[1]
    along_u = received.shape[3]
    along_v = received.shape[4]
    grid = dense_taps(assemble(received[0]), fine_weights, fine_bias)
    finer = dense_taps(split_halves(grid), coarse_weights, coarse_bias)
    grid = join_halves(finer, items)
    returned = lax.all_to_all(
        disassemble(grid, along_u, along_v), "space", split_axis=2, concat_axis=0, tiled=True
    )
    brick = fine_bricks(returned.reshape(cosets.shape))
    return brick.reshape(volume.shape)


def solution(mesh):
    return jax.shard_map(
        on_device,
        mesh=mesh,
        in_specs=(
            P("dp", "space", None, None, None, None),
            P(None, None, None, "dp", None),
            P(None, None, None, "dp", None),
            P(),
            P(),
        ),
        out_specs=P("dp", "space", None, None, None, None),
        check_vma=False,
    )
```

profile of v0, /device:TPU:1, one launch (start us, length us, event | category | flops | bytes accessed | tf_op | source)
XLA Modules:
  0.0 164.3 jit_solution(2453152711800644022)
XLA Ops:
  7.3 1.3 reshape_squeeze.60
  8.6 1.6 copy.22
  10.2 8.6 %all-to-all-start = ((bf16[32,2,1,2,4,4,256]{6,5,4,3,1,2,0:T(4,128)(2,1)}), bf16[32,2,1,2,4,4,256]{6,5,4,3,1,2,0:T(4,128)(2,1)S(1)}, u32[]{:S(2)}, u32[]{:S(2)}) async-start(bf16[32,2,1,2,4,4,256]{6,5,4,3,1,2,0:T(4,128)(2,1)} %bitcast.2), calls=%async_computation | async-start | bytes 2097152 | tf_op jit(solution)/shard_map/all_to_all | solution.py:91
  19.5 16.2 %all-to-all-done = bf16[32,2,1,2,4,4,256]{6,5,4,3,1,2,0:T(4,128)(2,1)S(1)} async-done(((bf16[32,2,1,2,4,4,256]{6,5,4,3,1,2,0:T(4,128)(2,1)}), bf16[32,2,1,2,4,4,256]{6,5,4,3,1,2,0:T(4,128)(2,1)S(1)}, u32[]{:S(2)}, u32[]{:S(2)}) %all-to-all-start) | async-done | bytes 1048608 | tf_op jit(solution)/shard_map/all_to_all | solution.py:91
  36.5 3.2 %pad_slice_fusion.27 = (bf16[2,16,16,4,256]{4,2,3,1,0:T(8,128)(2,1)}, bf16[2,16,16,4,256]{4,2,3,1,0:T(8,128)(2,1)}, bf16[2,16,16,4,256]{4,2,3,1,0:T(8,128)(2,1)}...) fusion(bf16[2,16,16,4,256]{4,2,3,1,0:T(8,128)(2,1)S(1)} %reshape.19), kind=kLoop, calls=%fused_computation.27 | loop fusion | bytes 8388608 | tf_op jit(solution)/shard_map/slice | solution.py:22
  39.7 6.7 %pad_slice_fusion.28 = (bf16[2,16,16,4,256]{4,2,3,1,0:T(8,128)(2,1)S(1)}, bf16[2,16,16,4,256]{4,2,3,1,0:T(8,128)(2,1)}, bf16[2,16,16,4,256]{4,2,3,1,0:T(8,128)(2...) fusion(bf16[2,16,16,4,256]{4,2,3,1,0:T(8,128)(2,1)S(1)} %reshape.19), kind=kLoop, calls=%fused_computation.28 | loop fusion | bytes 20971520 | tf_op jit(solution)/shard_map/slice | solution.py:22
  46.5 14.9 %all-gather.3.cloned.1.call-done = bf16[3,3,3,256,256]{4,3,2,1,0:T(8,128)(2,1)} async-done(((bf16[3,3,3,32,256]{4,3,2,1,0:T(8,128)(2,1)}), bf16[3,3,3,256,256]{4,3,2,1,0:T(8,128)(2,1)}) %all-gather.3.cloned.1.call-update) | async-done | bytes 3538960 | tf_op jit(solution)/shard_map/all_gather | solution.py:11
  61.4 2.3 %fusion.149 = (bf16[1,1,3,256,256]{4,3,2,1,0:T(8,128)(2,1)S(1)}, bf16[1,1,3,256,256]{4,3,2,1,0:T(8,128)(2,1)S(1)}, bf16[1,1,3,256,256]{4,3,2,1,0:T(8,128)(2,1)S(...) fusion(bf16[3,3,3,256,256]{4,3,2,1,0:T(8,128)(2,1)} %all-gather, ...), kind=kLoop, calls=%fused_computation.199 | loop fusion | bytes 7077888 | tf_op jit(solution)/shard_map/slice | solution.py:26
  64.0 1.2 fusion.24
  65.9 1.2 fusion.6
  67.7 1.2 fusion.12
  69.6 1.2 fusion.18
  71.4 1.2 fusion.30
  73.3 1.2 fusion
  74.8 1.2 fusion.36
  76.7 1.2 fusion.42
  78.2 2.1 %fusion.116 = bf16[2,16,16,4,256]{4,2,3,1,0:T(8,128)(2,1)S(1)} fusion(f32[2,16,16,4,256]{4,2,3,1,0:T(8,128)S(1)} %fusion.42, f32[2,16,16,4,256]{4,2,3,1,0:T(8,128)S(1)} %fusion.36, f32[2,16,16,4,256]{4,2,3,1,0:T(8,128)S(1)} %fusion.30, f32[2,16,16,4,256]{4,2,3,1,0:T(8,128)S(1)} %fusion.24, f32[2,16,16,4,256]{4,2,3,1,0:T(8,128)S(1)} %fusion.18, ...), kind=kOutput, calls=%fused_computation.170 | convolution fusion | flops 825229312 | bytes 22414336 | tf_op jit(solution)/shard_map/dot_general | solution.py:24
  81.0 2.8 %pad_slice_fusion.1 = (bf16[16,8,8,2,256]{4,2,3,1,0:T(8,128)(2,1)S(1)}, bf16[16,8,8,2,256]{4,2,3,1,0:T(8,128)(2,1)}, bf16[16,8,8,2,256]{4,2,3,1,0:T(8,128)(2,1)}...) fusion(bf16[16,8,8,2,256]{4,2,3,1,0:T(8,128)(2,1)S(1)} %bitcast.145), kind=kLoop, calls=%fused_computation.1 | loop fusion | bytes 8388608 | tf_op jit(solution)/shard_map/slice | solution.py:22
  83.8 6.5 %pad_slice_fusion.2 = (bf16[16,8,8,2,256]{4,2,3,1,0:T(8,128)(2,1)S(1)}, bf16[16,8,8,2,256]{4,2,3,1,0:T(8,128)(2,1)}, bf16[16,8,8,2,256]{4,2,3,1,0:T(8,128)(2,1)}...) fusion(bf16[16,8,8,2,256]{4,2,3,1,0:T(8,128)(2,1)S(1)} %bitcast.146), kind=kLoop, calls=%fused_computation.2 | loop fusion | bytes 20971520 | tf_op jit(solution)/shard_map/slice | solution.py:22
  90.3 20.1 %all-gather.5.cloned.1.call-done = bf16[3,3,3,256,256]{4,3,2,1,0:T(8,128)(2,1)} async-done(((bf16[3,3,3,32,256]{4,3,2,1,0:T(8,128)(2,1)}), bf16[3,3,3,256,256]{4,3,2,1,0:T(8,128)(2,1)}) %all-gather.5.cloned.1.call-update) | async-done | bytes 3538960 | tf_op jit(solution)/shard_map/all_gather | solution.py:11
  110.4 2.4 %fusion.148 = (bf16[1,1,3,256,256]{4,3,2,1,0:T(8,128)(2,1)S(1)}, bf16[1,1,3,256,256]{4,3,2,1,0:T(8,128)(2,1)S(1)}, bf16[1,1,3,256,256]{4,3,2,1,0:T(8,128)(2,1)S(...) fusion(bf16[3,3,3,256,256]{4,3,2,1,0:T(8,128)(2,1)} %all-gather, ...), kind=kLoop, calls=%fused_computation.198 | loop fusion | bytes 7077888 | tf_op jit(solution)/shard_map/slice | solution.py:26
  113.0 1.2 fusion.78
  114.9 1.2 fusion.60
  116.8 1.2 fusion.54
  118.6 1.2 fusion.66
  120.5 1.2 fusion.72
  122.3 1.2 fusion.84
  124.2 1.2 fusion.90
  126.0 1.2 fusion.96
  127.3 2.3 %fusion.125 = bf16[16,8,8,2,256]{4,2,3,1,0:T(8,128)(2,1)S(1)} fusion(f32[16,8,8,2,256]{4,2,3,1,0:T(8,128)S(1)} %fusion.96, f32[16,8,8,2,256]{4,2,3,1,0:T(8,128)S(1)} %fusion.90, f32[16,8,8,2,256]{4,2,3,1,0:T(8,128)S(1)} %fusion.84, f32[16,8,8,2,256]{4,2,3,1,0:T(8,128)S(1)} %fusion.78, f32[16,8,8,2,256]{4,2,3,1,0:T(8,128)S(1)} %fusion.72, ...), kind=kOutput, calls=%fused_computation.179 | convolution fusion | flops 825229312 | bytes 22414336 | tf_op jit(solution)/shard_map/dot_general | solution.py:24
  130.6 24.4 %all_to_all.30 = bf16[1,2,32,2,4,4,256]{6,5,4,3,1,0,2:T(4,128)(2,1)S(1)} all-to-all(bf16[1,2,32,2,4,4,256]{6,5,4,3,1,0,2:T(4,128)(2,1)S(1)} %bitcast.153), channel_id=1, replica_groups=mesh['dp'=8,'space'=32] {'space'}, dimensions={2} | all-to-all | bytes 2097152 | tf_op jit(solution)/shard_map/all_to_all | solution.py:98
  155.0 1.4 copy.30
  (111 shorter events, 14.7 us)
Async XLA Ops:
  6.5 54.9 %all-gather.3.cloned.1.call-start = ((), (), s32[]{:S(2)}) async-start(), calls=%async_computation.2 | async-start | bytes 3981312 | tf_op jit(solution)/shard_map/all_gather | solution.py:11
  10.2 25.5 %all-to-all-start = ((bf16[32,2,1,2,4,4,256]{6,5,4,3,1,2,0:T(4,128)(2,1)}), bf16[32,2,1,2,4,4,256]{6,5,4,3,1,2,0:T(4,128)(2,1)S(1)}, u32[]{:S(2)}, u32[]{:S(2)}) async-start(bf16[32,2,1,2,4,4,256]{6,5,4,3,1,2,0:T(4,128)(2,1)} %bitcast.2), calls=%async_computation | async-start | bytes 2097152 | tf_op jit(solution)/shard_map/all_to_all | solution.py:91
  18.8 91.7 %all-gather.5.cloned.1.call-start = ((), (), s32[]{:S(2)}) async-start(), calls=%async_computation.3 | async-start | bytes 3981312 | tf_op jit(solution)/shard_map/all_gather | solution.py:11
  61.4 2.3 %copy-start.34 = (bf16[2,16,16,4,256]{4,2,3,1,0:T(8,128)(2,1)S(1)}, bf16[2,16,16,4,256]{4,2,3,1,0:T(8,128)(2,1)}, u32[]{:S(2)}) copy-start(bf16[2,16,16,4,256]{4,2,3,1,0:T(8,128)(2,1)} %get-tuple-element.61) | copy-start | bytes 3145732
  61.4 2.6 %copy-start.35 = (bf16[2,16,16,4,256]{4,2,3,1,0:T(8,128)(2,1)S(1)}, bf16[2,16,16,4,256]{4,2,3,1,0:T(8,128)(2,1)}, u32[]{:S(2)}) copy-start(bf16[2,16,16,4,256]{4,2,3,1,0:T(8,128)(2,1)} %get-tuple-element.62) | copy-start | bytes 3145732
  64.0 1.5 copy-start.29
  64.0 1.9 %copy-start.30 = (bf16[2,16,16,4,256]{4,2,3,1,0:T(8,128)(2,1)S(1)}, bf16[2,16,16,4,256]{4,2,3,1,0:T(8,128)(2,1)}, u32[]{:S(2)}) copy-start(bf16[2,16,16,4,256]{4,2,3,1,0:T(8,128)(2,1)} %get-tuple-element.54) | copy-start | bytes 3145732
  65.9 1.5 copy-start.26
  65.9 1.9 %copy-start.27 = (bf16[2,16,16,4,256]{4,2,3,1,0:T(8,128)(2,1)S(1)}, bf16[2,16,16,4,256]{4,2,3,1,0:T(8,128)(2,1)}, u32[]{:S(2)}) copy-start(bf16[2,16,16,4,256]{4,2,3,1,0:T(8,128)(2,1)} %get-tuple-element.57) | copy-start | bytes 3145732
  67.7 1.5 copy-start.21
  67.7 1.9 %copy-start.22 = (bf16[2,16,16,4,256]{4,2,3,1,0:T(8,128)(2,1)S(1)}, bf16[2,16,16,4,256]{4,2,3,1,0:T(8,128)(2,1)}, u32[]{:S(2)}) copy-start(bf16[2,16,16,4,256]{4,2,3,1,0:T(8,128)(2,1)} %get-tuple-element.60) | copy-start | bytes 3145732
  69.6 1.5 copy-start.15
  69.6 1.9 %copy-start.16 = (bf16[2,16,16,4,256]{4,2,3,1,0:T(8,128)(2,1)S(1)}, bf16[2,16,16,4,256]{4,2,3,1,0:T(8,128)(2,1)}, u32[]{:S(2)}) copy-start(bf16[2,16,16,4,256]{4,2,3,1,0:T(8,128)(2,1)} %get-tuple-element.65) | copy-start | bytes 3145732
  71.4 1.5 copy-start.7
  71.4 1.9 %copy-start.46 = (bf16[2,16,16,4,256]{4,2,3,1,0:T(8,128)(2,1)S(1)}, bf16[2,16,16,4,256]{4,2,3,1,0:T(8,128)(2,1)}, u32[]{:S(2)}) copy-start(bf16[2,16,16,4,256]{4,2,3,1,0:T(8,128)(2,1)} %get-tuple-element.74) | copy-start | bytes 3145732
  73.3 1.5 copy-start.44
  74.8 1.5 copy-start.39
  74.8 1.9 %copy-start.40 = (bf16[2,16,16,4,256]{4,2,3,1,0:T(8,128)(2,1)S(1)}, bf16[2,16,16,4,256]{4,2,3,1,0:T(8,128)(2,1)}, u32[]{:S(2)}) copy-start(bf16[2,16,16,4,256]{4,2,3,1,0:T(8,128)(2,1)} %get-tuple-element.72) | copy-start | bytes 3145732
  76.7 1.5 copy-start.1
  76.7 1.5 copy-start.48
  110.4 2.4 %copy-start.36 = (bf16[16,8,8,2,256]{4,2,3,1,0:T(8,128)(2,1)S(1)}, bf16[16,8,8,2,256]{4,2,3,1,0:T(8,128)(2,1)}, u32[]{:S(2)}) copy-start(bf16[16,8,8,2,256]{4,2,3,1,0:T(8,128)(2,1)} %get-tuple-element.35) | copy-start | bytes 3145732
  110.4 2.6 %copy-start.37 = (bf16[16,8,8,2,256]{4,2,3,1,0:T(8,128)(2,1)S(1)}, bf16[16,8,8,2,256]{4,2,3,1,0:T(8,128)(2,1)}, u32[]{:S(2)}) copy-start(bf16[16,8,8,2,256]{4,2,3,1,0:T(8,128)(2,1)} %get-tuple-element.36) | copy-start | bytes 3145732
  113.0 1.5 copy-start.32
  113.0 1.9 %copy-start.33 = (bf16[16,8,8,2,256]{4,2,3,1,0:T(8,128)(2,1)S(1)}, bf16[16,8,8,2,256]{4,2,3,1,0:T(8,128)(2,1)}, u32[]{:S(2)}) copy-start(bf16[16,8,8,2,256]{4,2,3,1,0:T(8,128)(2,1)} %get-tuple-element.28) | copy-start | bytes 3145732
  114.9 1.5 copy-start.24
  114.9 1.9 %copy-start.47 = (bf16[16,8,8,2,256]{4,2,3,1,0:T(8,128)(2,1)S(1)}, bf16[16,8,8,2,256]{4,2,3,1,0:T(8,128)(2,1)}, u32[]{:S(2)}) copy-start(bf16[16,8,8,2,256]{4,2,3,1,0:T(8,128)(2,1)} %get-tuple-element.48) | copy-start | bytes 3145732
  116.8 1.5 copy-start.18
  116.8 1.9 %copy-start.19 = (bf16[16,8,8,2,256]{4,2,3,1,0:T(8,128)(2,1)S(1)}, bf16[16,8,8,2,256]{4,2,3,1,0:T(8,128)(2,1)}, u32[]{:S(2)}) copy-start(bf16[16,8,8,2,256]{4,2,3,1,0:T(8,128)(2,1)} %get-tuple-element.31) | copy-start | bytes 3145732
  118.6 1.9 %copy-start.13 = (bf16[16,8,8,2,256]{4,2,3,1,0:T(8,128)(2,1)S(1)}, bf16[16,8,8,2,256]{4,2,3,1,0:T(8,128)(2,1)}, u32[]{:S(2)}) copy-start(bf16[16,8,8,2,256]{4,2,3,1,0:T(8,128)(2,1)} %get-tuple-element.34) | copy-start | bytes 3145732
  120.5 1.9 %copy-start.10 = (bf16[16,8,8,2,256]{4,2,3,1,0:T(8,128)(2,1)S(1)}, bf16[16,8,8,2,256]{4,2,3,1,0:T(8,128)(2,1)}, u32[]{:S(2)}) copy-start(bf16[16,8,8,2,256]{4,2,3,1,0:T(8,128)(2,1)} %get-tuple-element.39) | copy-start | bytes 3145732
  122.3 1.9 %copy-start.45 = (bf16[16,8,8,2,256]{4,2,3,1,0:T(8,128)(2,1)S(1)}, bf16[16,8,8,2,256]{4,2,3,1,0:T(8,128)(2,1)}, u32[]{:S(2)}) copy-start(bf16[16,8,8,2,256]{4,2,3,1,0:T(8,128)(2,1)} %get-tuple-element.43) | copy-start | bytes 3145732
  124.2 1.9 %copy-start.43 = (bf16[16,8,8,2,256]{4,2,3,1,0:T(8,128)(2,1)S(1)}, bf16[16,8,8,2,256]{4,2,3,1,0:T(8,128)(2,1)}, u32[]{:S(2)}) copy-start(bf16[16,8,8,2,256]{4,2,3,1,0:T(8,128)(2,1)} %get-tuple-element.46) | copy-start | bytes 3145732
  (21 other events, 27.0 us)
Sparse Core Ops, SparseCore 0:
  9.1 52.2 all-gather.2
  63.2 47.2 all-gather.4
where the time goes:
time: 165 us; the launch traced here: 164 us
  waiting for transfers between devices  52.6 us (32%)
  local copies, waits for them, and re-layouts  41.6 us (25%)
  blocking collectives  24.4 us (15%)
  matrix products  23.4 us (14%)
  between operations  13.7 us (8%)
  starting transfers between devices  8.62 us (5%)
    all_gather x2, waiting for transfers between devices, filters(): return lax.all_gather(shard, 'dp', axis=3, tiled=True)  35 us
    all_to_all x1, blocking collectives, on_device(): lax.all_to_all(disassemble(grid, along_u, along_v), 'space', split_axis=2...  24.4 us
    dot_general x18, matrix products, dense_taps(): jnp.dot(stacked, weights[step_x, step_y].reshape(3 * channels, channels),...  23.4 us
    slice x4, local copies, waits for them, and re-layouts, dense_taps(): window[:, :, :, depth:depth + length_z]  19.3 us
    all_to_all x1, waiting for transfers between devices, on_device(): lax.all_to_all(outgoing, 'space', split_axis=0, concat_axis=2, tiled=True)  16.2 us
    unnamed x100, local copies, waits for them, and re-layouts  9.78 us
    all_to_all x1, starting transfers between devices, on_device(): lax.all_to_all(outgoing, 'space', split_axis=0, concat_axis=2, tiled=True)  8.58 us
    slice x2, local copies, waits for them, and re-layouts, dense_taps(): weights[step_x, step_y].reshape(3 * channels, channels)  4.72 us
  transfers between devices with their start and end apart: 3, of which 3 were waited for; matrix products, arithmetic and copies ran while one was open for 23% of the time, Pallas kernels for 0%

commit v1 on v0

--- a/solution.py
+++ b/solution.py
@@ -8,7 +8,12 @@
 
 
 def filters(shard):
-    return lax.all_gather(shard, "dp", axis=3, tiled=True)
+
+    def choose_frame(local_block):
+        res = jnp.stack([local_block] * lax.axis_size("dp"), axis=0)
+        return jnp.concatenate(lax.all_to_all(res, "dp", 0, 0), axis=3)
+
+    return choose_frame(shard)
 
 
 def dense_taps(grid, weights, bias):

time: 165 us -> 253 us (1.53)
  waiting for transfers between devices: 52.6 us -> 122 us
  blocking collectives: 24.4 us -> 46 us
  between operations: 13.7 us -> 0.36 us
  local copies, waits for them, and re-layouts: 41.6 us -> 46.1 us
  starting transfers between devices: 8.62 us -> 12.8 us
    all_to_all x1 -> x2, waiting for transfers between devices: 16.2 us -> 122 us  [choose_frame(): return jnp.concatenate(lax.all_to_all(res, 'dp', 0, 0), axis=3)]
    all_gather x2 -> x0, waiting for transfers between devices: 35 us -> none  [filters(): return lax.all_gather(shard, 'dp', axis=3, tiled=True)]
    all_to_all x0 -> x1, blocking collectives: none -> 25.3 us  [on_device(): lax.all_to_all(outgoing, 'space', split_axis=0, concat_axis=2, tiled=True)]
    all_to_all x0 -> x2, local copies, waits for them, and re-layouts: none -> 4.78 us  [choose_frame(): return jnp.concatenate(lax.all_to_all(res, 'dp', 0, 0), axis=3)]
    another operation x0 -> x2, local copies, waits for them, and re-layouts: none -> 4.43 us  [choose_frame(): res = jnp.stack([local_block] * lax.axis_size('dp'), axis=0)]
    all_to_all x1 -> x2, starting transfers between devices: 8.58 us -> 12.8 us  [choose_frame(): return jnp.concatenate(lax.all_to_all(res, 'dp', 0, 0), axis=3)]
    slice x2, local copies, waits for them, and re-layouts: 4.72 us -> 0.53 us  [dense_taps(): weights[step_x, step_y].reshape(3 * channels, channels)]
    all_to_all x1, blocking collectives: 24.4 us -> 20.7 us  [on_device(): lax.all_to_all(disassemble(grid, along_u, along_v), 'space', split_axis=2...]
  transfers between devices with their start and end apart: 3 -> 2, of which waited for: 3 -> 2; matrix products, arithmetic and copies ran while one was open for 23% -> 14% of each run, Pallas kernels for 0% -> 0%
where the time goes in v1:
time: 253 us; the launch traced here: 251 us
  waiting for transfers between devices  122 us (48%)
  local copies, waits for them, and re-layouts  46.1 us (18%)
  blocking collectives  46 us (18%)
  matrix products  23.5 us (9%)
  starting transfers between devices  12.8 us (5%)
    all_to_all x2, waiting for transfers between devices, choose_frame(): return jnp.concatenate(lax.all_to_all(res, 'dp', 0, 0), axis=3)  122 us
    all_to_all x1, blocking collectives, on_device(): lax.all_to_all(outgoing, 'space', split_axis=0, concat_axis=2, tiled=True)  25.3 us
    dot_general x18, matrix products, dense_taps(): jnp.dot(stacked, weights[step_x, step_y].reshape(3 * channels, channels),...  23.5 us
    all_to_all x1, blocking collectives, on_device(): lax.all_to_all(disassemble(grid, along_u, along_v), 'space', split_axis=2...  20.7 us
    slice x4, local copies, waits for them, and re-layouts, dense_taps(): window[:, :, :, depth:depth + length_z]  18.7 us
    all_to_all x2, starting transfers between devices, choose_frame(): return jnp.concatenate(lax.all_to_all(res, 'dp', 0, 0), axis=3)  12.8 us
    unnamed x96, local copies, waits for them, and re-layouts  10.8 us
  transfers between devices with their start and end apart: 2, of which 2 were waited for; matrix products, arithmetic and copies ran while one was open for 14% of the time, Pallas kernels for 0%

profile of v1, /device:TPU:1, one launch (start us, length us, event | category | flops | bytes accessed | tf_op | source)
XLA Modules:
  0.0 251.0 jit_solution(16018811452094055711)
XLA Ops:
  0.0 1.4 reshape_squeeze.60
  2.0 25.3 %all_to_all.40 = bf16[32,2,1,2,4,4,256]{6,5,4,3,1,2,0:T(4,128)(2,1)S(1)} all-to-all(bf16[32,2,1,2,4,4,256]{6,5,4,3,1,2,0:T(4,128)(2,1)S(1)} %bitcast.159), channel_id=1, replica_groups=mesh['dp'=8,'space'=32] {'space'}, dimensions={0} | all-to-all | bytes 2097152 | tf_op jit(solution)/shard_map/all_to_all | solution.py:96
  27.3 2.2 stack.4
  29.5 8.2 %all-to-all-start.1 = ((bf16[8,3,3,3,32,256]{5,4,3,2,1,0:T(8,128)(2,1)}), bf16[8,3,3,3,32,256]{5,4,3,2,1,0:T(8,128)(2,1)}, u32[]{:S(2)}, u32[]{:S(2)}) async-start(bf16[8,3,3,3,32,256]{5,4,3,2,1,0:T(8,128)(2,1)} %stack.4), calls=%async_computation.1 | async-start | bytes 7077888 | tf_op jit(solution)/shard_map/all_to_all | solution.py:14
  38.6 82.0 %all-to-all-done.1 = bf16[8,3,3,3,32,256]{5,4,3,2,1,0:T(8,128)(2,1)} async-done(((bf16[8,3,3,3,32,256]{5,4,3,2,1,0:T(8,128)(2,1)}), bf16[8,3,3,3,32,256]{5,4,3,2,1,0:T(8,128)(2,1)}, u32[]{:S(2)}, u32[]{:S(2)}) %all-to-all-start.1) | async-done | bytes 3538976 | tf_op jit(solution)/shard_map/all_to_all | solution.py:14
  120.5 2.2 stack.5
  122.8 4.7 %all-to-all-start.2 = ((bf16[8,3,3,3,32,256]{5,4,3,2,1,0:T(8,128)(2,1)}), bf16[8,3,3,3,32,256]{5,4,3,2,1,0:T(8,128)(2,1)}, u32[]{:S(2)}, u32[]{:S(2)}) async-start(bf16[8,3,3,3,32,256]{5,4,3,2,1,0:T(8,128)(2,1)} %stack.5), calls=%async_computation.2 | async-start | bytes 7077888 | tf_op jit(solution)/shard_map/all_to_all | solution.py:14
  127.4 2.8 %pad_slice_fusion.27 = (bf16[2,16,16,4,256]{4,2,3,1,0:T(8,128)(2,1)S(1)}, bf16[2,16,16,4,256]{4,2,3,1,0:T(8,128)(2,1)}, bf16[2,16,16,4,256]{4,2,3,1,0:T(8,128)(2...) fusion(bf16[2,16,16,4,256]{4,2,3,1,0:T(8,128)(2,1)S(1)} %reshape.35), kind=kLoop, calls=%fused_computation.27 | loop fusion | bytes 8388608 | tf_op jit(solution)/shard_map/slice | solution.py:27
  130.2 6.5 %pad_slice_fusion.28 = (bf16[2,16,16,4,256]{4,2,3,1,0:T(8,128)(2,1)S(1)}, bf16[2,16,16,4,256]{4,2,3,1,0:T(8,128)(2,1)S(1)}, bf16[2,16,16,4,256]{4,2,3,1,0:T(8,12...) fusion(bf16[2,16,16,4,256]{4,2,3,1,0:T(8,128)(2,1)S(1)} %reshape.35), kind=kLoop, calls=%fused_computation.28 | loop fusion | bytes 20971520 | tf_op jit(solution)/shard_map/slice | solution.py:27
  136.7 2.4 copy.35
  140.7 1.2 fusion.24
  142.5 1.2 fusion.6
  144.4 1.2 fusion.12
  146.3 1.2 fusion.18
  148.1 1.2 fusion.30
  149.6 1.2 fusion
  150.9 1.2 fusion.36
  153.9 2.2 fusion.116
  156.7 2.8 %pad_slice_fusion.1 = (bf16[16,8,8,2,256]{4,2,3,1,0:T(8,128)(2,1)S(1)}, bf16[16,8,8,2,256]{4,2,3,1,0:T(8,128)(2,1)}, bf16[16,8,8,2,256]{4,2,3,1,0:T(8,128)(2,1)}...) fusion(bf16[16,8,8,2,256]{4,2,3,1,0:T(8,128)(2,1)S(1)} %bitcast.151), kind=kLoop, calls=%fused_computation.1 | loop fusion | bytes 8388608 | tf_op jit(solution)/shard_map/slice | solution.py:27
  159.5 6.6 %pad_slice_fusion.2 = (bf16[16,8,8,2,256]{4,2,3,1,0:T(8,128)(2,1)S(1)}, bf16[16,8,8,2,256]{4,2,3,1,0:T(8,128)(2,1)}, bf16[16,8,8,2,256]{4,2,3,1,0:T(8,128)(2,1)}...) fusion(bf16[16,8,8,2,256]{4,2,3,1,0:T(8,128)(2,1)S(1)} %bitcast.152), kind=kLoop, calls=%fused_computation.2 | loop fusion | bytes 20971520 | tf_op jit(solution)/shard_map/slice | solution.py:27
  166.1 40.2 %all-to-all-done.2 = bf16[8,3,3,3,32,256]{5,4,3,2,1,0:T(8,128)(2,1)} async-done(((bf16[8,3,3,3,32,256]{5,4,3,2,1,0:T(8,128)(2,1)}), bf16[8,3,3,3,32,256]{5,4,3,2,1,0:T(8,128)(2,1)}, u32[]{:S(2)}, u32[]{:S(2)}) %all-to-all-start.2) | async-done | bytes 3538976 | tf_op jit(solution)/shard_map/all_to_all | solution.py:14
  206.3 2.4 copy.37
  212.1 1.2 fusion.60
  213.9 1.2 fusion.54
  215.8 1.2 fusion.66
  217.7 1.2 fusion.72
  219.5 1.2 fusion.84
  221.4 1.2 fusion.90
  223.2 1.2 fusion.96
  224.4 2.3 fusion.125
  227.8 20.7 %all_to_all.41 = bf16[1,2,32,2,4,4,256]{6,5,4,3,1,0,2:T(4,128)(2,1)S(1)} all-to-all(bf16[1,2,32,2,4,4,256]{6,5,4,3,1,0,2:T(4,128)(2,1)S(1)} %bitcast.162), channel_id=1, replica_groups=mesh['dp'=8,'space'=32] {'space'}, dimensions={2} | all-to-all | bytes 2097152 | tf_op jit(solution)/shard_map/all_to_all | solution.py:103
  248.5 1.4 copy.41
  (108 shorter events, 17.8 us)
Async XLA Ops:
  0.0 27.3 %copy-start.44 = (bf16[3,3,3,32,256]{4,3,2,1,0:T(8,128)(2,1)S(1)}, bf16[3,3,3,32,256]{4,3,2,1,0:T(8,128)(2,1)}, u32[]{:S(2)}) copy-start(bf16[3,3,3,32,256]{4,3,2,1,0:T(8,128)(2,1)} %param.6) | copy-start | bytes 1327108
  29.5 91.0 %all-to-all-start.1 = ((bf16[8,3,3,3,32,256]{5,4,3,2,1,0:T(8,128)(2,1)}), bf16[8,3,3,3,32,256]{5,4,3,2,1,0:T(8,128)(2,1)}, u32[]{:S(2)}, u32[]{:S(2)}) async-start(bf16[8,3,3,3,32,256]{5,4,3,2,1,0:T(8,128)(2,1)} %stack.4), calls=%async_computation.1 | async-start | bytes 7077888 | tf_op jit(solution)/shard_map/all_to_all | solution.py:14
  37.7 82.8 %copy-start.45 = (bf16[3,3,3,32,256]{4,3,2,1,0:T(8,128)(2,1)S(1)}, bf16[3,3,3,32,256]{4,3,2,1,0:T(8,128)(2,1)}, u32[]{:S(2)}) copy-start(bf16[3,3,3,32,256]{4,3,2,1,0:T(8,128)(2,1)} %param.7) | copy-start | bytes 1327108
  122.8 83.5 %all-to-all-start.2 = ((bf16[8,3,3,3,32,256]{5,4,3,2,1,0:T(8,128)(2,1)}), bf16[8,3,3,3,32,256]{5,4,3,2,1,0:T(8,128)(2,1)}, u32[]{:S(2)}, u32[]{:S(2)}) async-start(bf16[8,3,3,3,32,256]{5,4,3,2,1,0:T(8,128)(2,1)} %stack.5), calls=%async_computation.2 | async-start | bytes 7077888 | tf_op jit(solution)/shard_map/all_to_all | solution.py:14
  139.1 1.2 copy-start.32
  139.1 1.5 copy-start.33
  140.7 1.5 copy-start.30
  140.7 1.9 copy-start.31
  142.5 1.5 copy-start.27
  142.5 1.9 copy-start.28
  144.4 1.5 copy-start.22
  144.4 1.9 copy-start.23
  146.3 1.5 copy-start.16
  146.3 1.9 copy-start.17
  148.1 1.5 copy-start.42
  150.9 1.5 copy-start.39
  150.9 1.9 copy-start.40
  208.7 1.5 copy-start.25
  210.2 1.5 copy-start.19
  210.2 1.9 copy-start.20
  212.1 1.5 copy-start.14
  212.1 1.9 copy-start.43
  213.9 1.5 copy-start.10
  213.9 1.9 copy-start.11
  215.8 1.5 copy-start.7
  215.8 1.9 copy-start.8
  217.6 1.5 copy-start.4
  217.7 1.9 copy-start.5
  219.5 1.5 copy-start.2
  219.5 1.9 copy-start.37
  221.4 1.5 copy-start.35
  221.4 1.9 copy-start.36
  (18 other events, 22.0 us)
